TPU v7x, 32 devices: a whole 2x2x4 slice. The times are simulated.
32 devices in a mesh: parts: 2 (over y), rows: 4 (over x, core), cols: 4 (over z).
Axes of the slice: x: 2, y: 2, z: 4, core: 2. Of those that a mesh axis runs over, the one named last changes fastest.
Arguments:
- pair: float32 [256, 4, 32, 128], P(('parts', 'rows'), None, 'cols'), parts along dimension 0, may hold values from -6 to 6
- singles: float32 [256, 384], P(('parts', 'rows')), parts along dimension 0, may hold values from -6 to 6
- restype: int32 [256], P(('parts', 'rows')), parts along dimension 0, may hold values from 0 to 31
- block_mask: int32 [32, 4, 4], P(('parts', 'rows'), None, 'cols'), parts along dimension 0, may hold values from 0 to 1, as said below
- ln_trans: float32 [128], replicated, may hold values from 0.1 to 1.9
- w_trans_in: bfloat16 [128, 1024], replicated, may hold values from -0.5 to 0.5
- w_trans_out: bfloat16 [512, 128], replicated, may hold values from -0.25 to 0.25
- ln_bias: float32 [128], replicated, may hold values from 0.1 to 1.9
- w_bias: bfloat16 [128, 16], replicated, may hold values from -0.5 to 0.5
- restype_table: float32 [32, 384], replicated, may hold values from -6 to 6
- ln_single: float32 [384], replicated, may hold values from 0.1 to 1.9
- w_attn: bfloat16 [384, 1536], replicated, may hold values from -80 to 80
- w_single_out: bfloat16 [384, 384], replicated, may hold values from -0.3125 to 0.3125
- w_dist: bfloat16 [128, 64], replicated, may hold values from -0.5 to 0.5
- dist_bias: float32 [64], replicated, may hold values from -6 to 6
Outputs:
- pair_next: float32 [256, 4, 32, 128], P(('parts', 'rows'), None, 'cols'), parts along dimension 0
- singles_next: float32 [256, 384], P(('parts', 'rows')), parts along dimension 0
- dist_logits: float32 [256, 4, 2048], P(('parts', 'rows'), None, 'cols'), parts along dimension 0
There are 2 independent parts, one for each index of `parts`. A program takes and returns all parts, laid end to end along the dimension named above; an argument that names none is the same for every part. Nothing has to cross between parts.
Inputs may be any that keep to these rules, and one draw needn't show every extreme that they name: block_mask[p, a, c] is 1 where p == a * 4 + c.
All inputs are finite; a program needn't handle non-finite values.
Results may differ from a plain program's by a relative error of at most 0.0044.
Values may be sent and summed in bfloat16 or wider, within the bound.
No kernel may reach another device: no remote copies, remote signals or barrier semaphores. Data moves between devices by JAX's collectives and lax.ppermute only.
A program may use at most 64 MiB of HBM per device.

v0:
```python
import math
import jax
import jax.numpy as jnp
from jax import lax
from jax.sharding import PartitionSpec as P

eps_norm = 1e-05


def layer_norm(values, gain_vec):
    average = jnp.mean(values, axis=-1, keepdims=True)
    centred = values - average
    spread = jnp.mean(centred * centred, axis=-1, keepdims=True)
    return centred * lax.rsqrt(spread + eps_norm) * gain_vec


def pair_block(pair_rows, ln_trans, w_trans_in, w_trans_out, ln_bias, w_bias, w_dist):
    hidden_units = w_trans_out.shape[0]
    normed = layer_norm(pair_rows, ln_trans).astype(jnp.bfloat16)
    gate_up = jnp.dot(normed, w_trans_in, preferred_element_type=jnp.float32)
    hidden = (jax.nn.silu(gate_up[:, :hidden_units]) * gate_up[:, hidden_units:]).astype(
        jnp.bfloat16
    )
    updated = pair_rows + jnp.dot(hidden, w_trans_out, preferred_element_type=jnp.float32)
    biased = layer_norm(updated, ln_bias).astype(jnp.bfloat16)
    head_bias = jnp.dot(biased, w_bias, preferred_element_type=jnp.float32)
    binned = jnp.dot(
        updated.astype(jnp.bfloat16), w_dist, preferred_element_type=jnp.float32
    ).astype(jnp.bfloat16)
    return (updated, head_bias, binned)


def local(
    pair,
    singles,
    restype,
    block_mask,
    ln_trans,
    w_trans_in,
    w_trans_out,
    ln_bias,
    w_bias,
    restype_table,
    ln_single,
    w_attn,
    w_single_out,
    w_dist,
    dist_bias,
):
    queries, key_groups, block_len, channels = pair.shape
    key_count = key_groups * block_len
    q_groups = queries // block_len
    head_count = w_bias.shape[1]
    model_width = w_single_out.shape[0]
    head_width = model_width // head_count
    bin_count = w_dist.shape[1]
    step_rows = math.gcd(queries, 16)
    pair_tiles = pair.reshape(queries // step_rows, step_rows * key_count, channels)

    def run_tile(pair_tile):
        return pair_block(pair_tile, ln_trans, w_trans_in, w_trans_out, ln_bias, w_bias, w_dist)

    updated, head_bias, binned = lax.map(run_tile, pair_tiles)
    pair_next = updated.reshape(queries, key_groups, block_len, channels)
    head_bias = head_bias.reshape(queries, key_count, head_count)
    binned = binned.reshape(queries, key_groups, block_len, bin_count)
    type_count = restype_table.shape[0]
    one_hot = (restype[:, None] == jnp.arange(type_count, dtype=jnp.int32)[None, :]).astype(
        jnp.float32
    )
    embedded = singles + jnp.dot(one_hot, restype_table, precision=lax.Precision.HIGHEST)
    normed_s = layer_norm(embedded, ln_single).astype(jnp.bfloat16)
    query_proj = (
        jnp.dot(normed_s, w_attn[:, :model_width], preferred_element_type=jnp.float32)
        * head_width ** (-0.5)
    ).astype(jnp.bfloat16)
    gate_vals = jax.nn.sigmoid(
        jnp.dot(normed_s, w_attn[:, 3 * model_width :], preferred_element_type=jnp.float32)
    )
    key_weights = w_attn[:, model_width : 3 * model_width]
    own_rows = lax.dynamic_slice_in_dim(normed_s, lax.axis_index("cols") * block_len, block_len, 0)
    local_kv = jnp.dot(own_rows, key_weights, preferred_element_type=jnp.float32).astype(
        jnp.bfloat16
    )
    key_values = lax.all_gather(local_kv, "rows", axis=0, tiled=True)
    q_heads = query_proj.reshape(queries, head_count, head_width)
    k_heads = key_values[:, :model_width].reshape(key_count, head_count, head_width)
    v_heads = key_values[:, model_width:].reshape(key_count, head_count, head_width)
    scores = jnp.einsum("qhd,khd->hqk", q_heads, k_heads, preferred_element_type=jnp.float32)
    scores = scores + jnp.transpose(head_bias, (2, 0, 1))
    allowed = (
        jnp.broadcast_to(
            block_mask[:, None, :, :], (q_groups, block_len, key_groups, block_len)
        ).reshape(queries, key_count)
        > 0
    )
    scores = jnp.where(allowed[None], scores, jnp.float32(-1000000000.0))
    local_max = jnp.max(scores, axis=-1)
    row_max = lax.pmax(local_max, "cols")
    expo = jnp.exp(scores - row_max[:, :, None])
    totals = jnp.sum(expo, axis=-1)
    weighted = jnp.einsum(
        "hqk,khd->qhd", expo.astype(jnp.bfloat16), v_heads, preferred_element_type=jnp.float32
    ).reshape(queries, model_width)
    totals, weighted = (
        lax.psum(totals.astype(jnp.bfloat16), "cols").astype(jnp.float32),
        lax.psum(weighted.astype(jnp.bfloat16), "cols").astype(jnp.float32),
    )
    normalised = (
        weighted.reshape(queries, head_count, head_width) / jnp.transpose(totals)[:, :, None]
    )
    attended = (gate_vals * normalised.reshape(queries, model_width)).astype(jnp.bfloat16)
    singles_next = embedded + jnp.dot(attended, w_single_out, preferred_element_type=jnp.float32)
    grouped = binned.reshape(q_groups, block_len, key_groups, block_len * bin_count)
    outgoing = jnp.transpose(grouped, (2, 0, 1, 3)).reshape(
        key_groups * q_groups, 1, block_len, block_len * bin_count
    )
    arrived = lax.all_to_all(outgoing, ("rows", "cols"), split_axis=0, concat_axis=1, tiled=True)
    mirrored = jnp.transpose(
        arrived.reshape(key_groups, q_groups, block_len, block_len, bin_count), (1, 3, 0, 2, 4)
    )
    mirrored = mirrored.reshape(queries, key_groups, block_len, bin_count)
    logits = binned.astype(jnp.float32) + mirrored.astype(jnp.float32) + dist_bias
    dist_logits = logits.reshape(queries, key_groups, block_len * bin_count)
    return (pair_next, singles_next, dist_logits)


def solution(mesh):
    return jax.shard_map(
        local,
        mesh=mesh,
        in_specs=(
            P(("parts", "rows"), None, "cols", None),
            P(("parts", "rows"), None),
            P(("parts", "rows")),
            P(("parts", "rows"), None, "cols"),
            P(),
            P(),
            P(),
            P(),
            P(),
            P(),
            P(),
            P(),
            P(),
            P(),
            P(),
        ),
        out_specs=(
            P(("parts", "rows"), None, "cols", None),
            P(("parts", "rows"), None),
            P(("parts", "rows"), None, "cols"),
        ),
        check_vma=False,
    )
```

profile of v0, /device:TPU:0, one launch (start us, length us, event | category | flops | bytes accessed | tf_op | source)
XLA Modules:
  0.0 56.2 jit_solution(419873935561623359)
XLA Ops:
  0.7 8.1 %while.14 = (s32[]{:T(128)}, f32[2,512,128]{2,1,0:T(8,128)S(1)}, f32[2,512,16]{1,0,2:T(2,128)S(1)}, bf16[2,512,64]{1,2,0:T(8,128)(2,1)S(1)}, f32[2,512,128]{2,1,...) while((s32[]{:T(128)}, f32[2,512,128]{2,1,0:T(8,128)S(1)}, ...), condition=%wide.region_5.6_spmd, body=%wide.region_0.5_spmd.sunk | while | flops 214598656 | bytes 10466621 | solution.py:63
  0.7 1.1 %fusion.65 = (f32[512]{0:T(512)S(1)}, f32[1,512,128]{2,1,0:T(8,128)S(1)}) fusion(f32[2,512,128]{2,1,0:T(8,128)} %get-tuple-element.248, s32[]{:T(128)S(6)} %copy.112), kind=kLoop, calls=%fused_computation.63.clone.1 | loop fusion | flops 65024 | bytes 526340 | tf_op jit(solution)/shard_map/while/body/eval_jaxpr/reduce_sum | solution.py:11
  2.1 0.5 fusion.66
  2.6 0.4 copy-done.14
  3.0 0.5 fusion.67
  3.7 0.4 copy-done.4
  4.1 0.2 convolution_bitcast_fusion.2
  4.8 1.1 %fusion.65 = (f32[512]{0:T(512)S(1)}, f32[1,512,128]{2,1,0:T(8,128)S(1)}) fusion(f32[2,512,128]{2,1,0:T(8,128)} %get-tuple-element.248, s32[]{:T(128)S(6)} %copy.112), kind=kLoop, calls=%fused_computation.63.clone.1 | loop fusion | flops 65024 | bytes 526340 | tf_op jit(solution)/shard_map/while/body/eval_jaxpr/reduce_sum | solution.py:11
  6.2 0.5 fusion.66
  6.7 0.4 copy-done.14
  7.0 0.5 fusion.67
  7.8 0.4 copy-done.4
  8.2 0.2 convolution_bitcast_fusion.2
  9.2 0.7 %copy.81 = bf16[4,4,8,512]{3,2,1,0:T(8,128)(2,1)} copy(bf16[4,4,8,512]{3,0,2,1:T(4,128)(2,1)S(1)} %bitcast.74) | data formatting | bytes 262144 | tf_op jit(solution)/shard_map/transpose | solution.py:115
  9.9 7.4 %all-to-all-start = ((bf16[16,1,8,512]{3,2,1,0:T(8,128)(2,1)}), bf16[16,1,8,512]{3,2,1,0:T(8,128)(2,1)S(1)}, u32[]{:S(2)}, u32[]{:S(2)}) async-start(bf16[16,1,8,512]{3,2,1,0:T(8,128)(2,1)} %bitcast.16), calls=%async_computation | async-start | bytes 262144 | tf_op jit(solution)/shard_map/all_to_all | solution.py:118
  17.3 0.3 fusion.38
  18.7 5.3 %all_gather.3 = bf16[32,768]{1,0:T(8,128)(2,1)S(1)} all-gather(bf16[8,768]{1,0:T(8,128)(2,1)S(1)} %convolution_convert_fusion.2), channel_id=1, replica_groups=mesh['parts'=2,'rows'=4,'cols'=4] {'rows'}, dimensions={0}, use_global_device_ids=true | all-gather | bytes 61440 | tf_op jit(solution)/shard_map/all_gather | solution.py:85
  24.5 0.3 fusion.39
  24.8 12.1 %pmax.7 = f32[16,32]{1,0:T(8,128)S(1)} all-reduce(f32[16,32]{1,0:T(8,128)S(1)} %get-tuple-element.141), channel_id=1, replica_groups=mesh['parts'=2,'rows'=4,'cols'=4] {'cols'}, use_global_device_ids=true, to_apply=%region_9.10 | all-reduce | flops 512 | bytes 4096 | tf_op jit(solution)/shard_map/pmax | solution.py:99
  37.0 0.2 convolution_convert_fusion.1
  37.6 15.8 %all-reduce = (bf16[32,16]{0,1:T(8,128)(2,1)S(1)}, bf16[32,384]{1,0:T(8,128)(2,1)S(1)}) all-reduce(bf16[32,16]{0,1:T(8,128)(2,1)S(1)} %bitcast.79, bf16[32,384]{1,0:T(8,128)(2,1)S(1)} %copy.89), channel_id=1, replica_groups=mesh['parts'=2,'rows'=4,'cols'=4] {'cols'}, use_global_device_ids=true, to_apply=%region_12.13 | all-reduce | flops 12800 | bytes 51200 | tf_op jit(solution)/shard_map/psum | solution.py:106
  53.7 0.2 reshape.110
  54.0 1.0 %convolution_add_fusion.3 = f32[32,384]{1,0:T(8,128)} fusion(f32[32,384]{1,0:T(8,128)S(1)} %get-tuple-element.140, bf16[384,384]{1,0:T(8,128)(2,1)S(1)} %copy-done, bf16[32,384]{1,0:T(8,128)(2,1)S(1)} %multiply_convert_fusion.4, bf16[384,1536]{1,0:T(8,128)(2,1)S(1)} %copy-done.2, f32[32,384]{1,0:T(8,128)S(1)} %div.40, ...), kind=kOutput, calls=%fused_computation.36 | convolution fusion | flops 18972672 | bytes 786432 | tf_op jit(solution)/shard_map/dot_general | solution.py:113
  55.4 0.8 %add_add_fusion = f32[32,4,512]{2,1,0:T(4,128)} fusion(f32[32,4,512]{2,1,0:T(4,128)S(1)} %reshape.110, f32[32,4,512]{2,1,0:T(4,128)S(1)} %reshape.111, f32[512]{0:T(512)S(1)} %add.82), kind=kLoop, calls=%fused_computation.44 | loop fusion | flops 131072 | bytes 788480 | tf_op jit(solution)/shard_map/add | solution.py:123
  (95 shorter events, 4.7 us)
Async XLA Ops:
  0.6 53.4 %copy-start = (bf16[384,384]{1,0:T(8,128)(2,1)S(1)}, bf16[384,384]{1,0:T(8,128)(2,1)}, u32[]{:S(2)}) copy-start(bf16[384,384]{1,0:T(8,128)(2,1)} %param.29) | copy-start | bytes 884740
  0.7 1.4 %copy-start.1 = (bf16[128,1024]{1,0:T(8,128)(2,1)S(1)}, bf16[128,1024]{1,0:T(8,128)(2,1)}, u32[]{:S(2)}) copy-start(bf16[128,1024]{1,0:T(8,128)(2,1)} %get-tuple-element.250) | copy-start | bytes 786436 | tf_op jit(solution)/shard_map/while
  0.7 1.4 %copy-start.8 = (f32[128]{0:T(128)S(1)}, f32[128]{0:T(128)}, u32[]{:S(2)}) copy-start(f32[128]{0:T(128)} %get-tuple-element.249) | copy-start | bytes 1540 | tf_op jit(solution)/shard_map/while
  2.1 0.9 %copy-start.14 = (bf16[512,128]{1,0:T(8,128)(2,1)S(1)}, bf16[512,128]{1,0:T(8,128)(2,1)}, u32[]{:S(2)}) copy-start(bf16[512,128]{1,0:T(8,128)(2,1)} %get-tuple-element.251) | copy-start | bytes 393220 | tf_op jit(solution)/shard_map/while
  3.5 0.7 %copy-start.4 = (bf16[128,16]{0,1:T(8,128)(2,1)S(1)}, bf16[128,16]{0,1:T(8,128)(2,1)}, u32[]{:S(2)}) copy-start(bf16[128,16]{0,1:T(8,128)(2,1)} %get-tuple-element.253) | copy-start | bytes 12292 | tf_op jit(solution)/shard_map/while
  3.5 0.7 %copy-start.7 = (f32[128]{0:T(128)S(1)}, f32[128]{0:T(128)}, u32[]{:S(2)}) copy-start(f32[128]{0:T(128)} %get-tuple-element.252) | copy-start | bytes 1540 | tf_op jit(solution)/shard_map/while
  3.5 1.1 %copy-start.3 = (bf16[128,64]{0,1:T(8,128)(2,1)S(1)}, bf16[128,64]{0,1:T(8,128)(2,1)}, u32[]{:S(2)}) copy-start(bf16[128,64]{0,1:T(8,128)(2,1)} %get-tuple-element.254) | copy-start | bytes 49156 | tf_op jit(solution)/shard_map/while
  4.7 1.4 %copy-start.1 = (bf16[128,1024]{1,0:T(8,128)(2,1)S(1)}, bf16[128,1024]{1,0:T(8,128)(2,1)}, u32[]{:S(2)}) copy-start(bf16[128,1024]{1,0:T(8,128)(2,1)} %get-tuple-element.250) | copy-start | bytes 786436 | tf_op jit(solution)/shard_map/while
  4.8 1.4 %copy-start.8 = (f32[128]{0:T(128)S(1)}, f32[128]{0:T(128)}, u32[]{:S(2)}) copy-start(f32[128]{0:T(128)} %get-tuple-element.249) | copy-start | bytes 1540 | tf_op jit(solution)/shard_map/while
  6.1 0.9 %copy-start.14 = (bf16[512,128]{1,0:T(8,128)(2,1)S(1)}, bf16[512,128]{1,0:T(8,128)(2,1)}, u32[]{:S(2)}) copy-start(bf16[512,128]{1,0:T(8,128)(2,1)} %get-tuple-element.251) | copy-start | bytes 393220 | tf_op jit(solution)/shard_map/while
  7.5 0.7 %copy-start.4 = (bf16[128,16]{0,1:T(8,128)(2,1)S(1)}, bf16[128,16]{0,1:T(8,128)(2,1)}, u32[]{:S(2)}) copy-start(bf16[128,16]{0,1:T(8,128)(2,1)} %get-tuple-element.253) | copy-start | bytes 12292 | tf_op jit(solution)/shard_map/while
  7.5 0.7 %copy-start.7 = (f32[128]{0:T(128)S(1)}, f32[128]{0:T(128)}, u32[]{:S(2)}) copy-start(f32[128]{0:T(128)} %get-tuple-element.252) | copy-start | bytes 1540 | tf_op jit(solution)/shard_map/while
  7.5 1.1 %copy-start.3 = (bf16[128,64]{0,1:T(8,128)(2,1)S(1)}, bf16[128,64]{0,1:T(8,128)(2,1)}, u32[]{:S(2)}) copy-start(bf16[128,64]{0,1:T(8,128)(2,1)} %get-tuple-element.254) | copy-start | bytes 49156 | tf_op jit(solution)/shard_map/while
  8.8 9.4 %copy-start.13 = (f32[2,512,128]{2,1,0:T(8,128)}, f32[2,512,128]{2,1,0:T(8,128)S(1)}, u32[]{:S(2)}) copy-start(f32[2,512,128]{2,1,0:T(8,128)S(1)} %get-tuple-element.62) | copy-start | bytes 1572868
  8.8 8.5 %copy-start.5 = (f32[32,384]{1,0:T(8,128)S(1)}, f32[32,384]{1,0:T(8,128)}, u32[]{:S(2)}) copy-start(f32[32,384]{1,0:T(8,128)} %param.18) | copy-start | bytes 147460
  8.8 8.5 %copy-start.6 = (f32[32,384]{1,0:T(8,128)S(1)}, f32[32,384]{1,0:T(8,128)}, u32[]{:S(2)}) copy-start(f32[32,384]{1,0:T(8,128)} %param.26) | copy-start | bytes 147460
  8.8 8.5 %copy-start.11 = (s32[32]{0:T(128)S(1)}, s32[32]{0:T(128)}, u32[]{:S(2)}) copy-start(s32[32]{0:T(128)} %param.19) | copy-start | bytes 388
  8.8 9.3 %copy-start.9 = (f32[384]{0:T(512)S(1)}, f32[384]{0:T(512)}, u32[]{:S(2)}) copy-start(f32[384]{0:T(512)} %param.27) | copy-start | bytes 4612
  8.8 9.4 %copy-start.2 = (bf16[384,1536]{1,0:T(8,128)(2,1)S(1)}, bf16[384,1536]{1,0:T(8,128)(2,1)}, u32[]{:S(2)}) copy-start(bf16[384,1536]{1,0:T(8,128)(2,1)} %param.28) | copy-start | bytes 3538948
  9.9 45.1 %all-to-all-start = ((bf16[16,1,8,512]{3,2,1,0:T(8,128)(2,1)}), bf16[16,1,8,512]{3,2,1,0:T(8,128)(2,1)S(1)}, u32[]{:S(2)}, u32[]{:S(2)}) async-start(bf16[16,1,8,512]{3,2,1,0:T(8,128)(2,1)} %bitcast.16), calls=%async_computation | async-start | bytes 262144 | tf_op jit(solution)/shard_map/all_to_all | solution.py:118
  17.6 6.6 %copy-start.10 = (s32[4,4,1]{1,2,0:T(1,128)S(1)}, s32[4,4,1]{1,2,0:T(1,128)}, u32[]{:S(2)}) copy-start(s32[4,4,1]{1,2,0:T(1,128)} %param.20) | copy-start | bytes 196
  37.3 16.7 %copy-start.12 = (f32[64]{0:T(128)S(1)}, f32[64]{0:T(128)}, u32[]{:S(2)}) copy-start(f32[64]{0:T(128)} %param.31) | copy-start | bytes 772
where the time goes:
time: 56.6 us; the launch traced here: 56.2 us
  blocking collectives  33.3 us (59%)
  starting transfers between devices  7.39 us (13%)
  local copies, waits for them, and re-layouts  5.89 us (10%)
  matrix products  4.73 us (8%)
  other arithmetic  3.66 us (6%)
  between operations  0.96 us (2%)
    psum x1, blocking collectives, local(): lax.psum(totals.astype(jnp.bfloat16), 'cols').astype(jnp.float32)  15.8 us
    pmax x1, blocking collectives, local(): row_max = lax.pmax(local_max, 'cols')  12.1 us
    all_to_all x1, starting transfers between devices, local(): lax.all_to_all(outgoing, ('rows', 'cols'), split_axis=0, concat_axis=1, t...  7.39 us
    all_gather x1, blocking collectives, local(): key_values = lax.all_gather(local_kv, 'rows', axis=0, tiled=True)  5.33 us
    reduce_sum x2, other arithmetic, layer_norm(): average = jnp.mean(values, axis=-1, keepdims=True)  2.28 us
    while x24, local copies, waits for them, and re-layouts  1.65 us
  transfers between devices with their start and end apart: 1, of which 0 were waited for; matrix products, arithmetic and copies ran while one was open for 7% of the time, Pallas kernels for 0%

commit v1 on v0

--- a/solution.py
+++ b/solution.py
@@ -5,6 +5,11 @@
 from jax.sharding import PartitionSpec as P
 
 eps_norm = 1e-05
+
+
+def gather_and_add(x, name):
+    terms = lax.all_gather(x, name)
+    return jnp.sum(terms, axis=0)
 
 
 def layer_norm(values, gain_vec):
@@ -103,7 +108,7 @@
         "hqk,khd->qhd", expo.astype(jnp.bfloat16), v_heads, preferred_element_type=jnp.float32
     ).reshape(queries, model_width)
     totals, weighted = (
-        lax.psum(totals.astype(jnp.bfloat16), "cols").astype(jnp.float32),
+        gather_and_add(totals.astype(jnp.bfloat16), "cols").astype(jnp.float32),
         lax.psum(weighted.astype(jnp.bfloat16), "cols").astype(jnp.float32),
     )
     normalised = (

time: 56.6 us -> 69.8 us (1.23)
  blocking collectives: 33.3 us -> 46.5 us
    all_gather x0 -> x1, blocking collectives: none -> 13.2 us  [gather_and_add(): terms = lax.all_gather(x, name)]
  transfers between devices with their start and end apart: 1 -> 1, of which waited for: 0 -> 0; matrix products, arithmetic and copies ran while one was open for 7% -> 6% of each run, Pallas kernels for 0% -> 0%
where the time goes in v1:
time: 69.8 us; the launch traced here: 69.4 us
  blocking collectives  46.5 us (67%)
  starting transfers between devices  7.39 us (11%)
  local copies, waits for them, and re-layouts  5.89 us (8%)
  matrix products  4.74 us (7%)
  other arithmetic  3.67 us (5%)
  between operations  0.97 us (1%)
    psum x1, blocking collectives, local(): lax.psum(weighted.astype(jnp.bfloat16), 'cols').astype(jnp.float32)  15.8 us
    all_gather x1, blocking collectives, gather_and_add(): terms = lax.all_gather(x, name)  13.2 us
    pmax x1, blocking collectives, local(): row_max = lax.pmax(local_max, 'cols')  12.1 us
    all_to_all x1, starting transfers between devices, local(): lax.all_to_all(outgoing, ('rows', 'cols'), split_axis=0, concat_axis=1, t...  7.39 us
    all_gather x1, blocking collectives, local(): key_values = lax.all_gather(local_kv, 'rows', axis=0, tiled=True)  5.33 us
    reduce_sum x2, other arithmetic, layer_norm(): average = jnp.mean(values, axis=-1, keepdims=True)  2.28 us
    while x24, local copies, waits for them, and re-layouts  1.65 us
  transfers between devices with their start and end apart: 1, of which 0 were waited for; matrix products, arithmetic and copies ran while one was open for 6% of the time, Pallas kernels for 0%

profile of v1, /device:TPU:0, one launch (start us, length us, event | category | flops | bytes accessed | tf_op | source)
XLA Modules:
  0.0 69.4 jit_solution(15048913761642670604)
XLA Ops:
  0.7 8.1 %while.14 = (s32[]{:T(128)}, f32[2,512,128]{2,1,0:T(8,128)S(1)}, f32[2,512,16]{1,0,2:T(2,128)S(1)}, bf16[2,512,64]{1,2,0:T(8,128)(2,1)S(1)}, f32[2,512,128]{2,1,...) while((s32[]{:T(128)}, f32[2,512,128]{2,1,0:T(8,128)S(1)}, ...), condition=%wide.region_5.6_spmd, body=%wide.region_0.5_spmd.sunk | while | flops 214598656 | bytes 10466621 | solution.py:68
  0.7 1.1 %fusion.65 = (f32[512]{0:T(512)S(1)}, f32[1,512,128]{2,1,0:T(8,128)S(1)}) fusion(f32[2,512,128]{2,1,0:T(8,128)} %get-tuple-element.246, s32[]{:T(128)S(6)} %copy.112), kind=kLoop, calls=%fused_computation.63.clone.1 | loop fusion | flops 65024 | bytes 526340 | tf_op jit(solution)/shard_map/while/body/eval_jaxpr/reduce_sum | solution.py:16
  2.1 0.5 fusion.66
  2.6 0.4 copy-done.14
  3.0 0.5 fusion.67
  3.7 0.4 copy-done.4
  4.1 0.2 convolution_bitcast_fusion.2
  4.8 1.1 %fusion.65 = (f32[512]{0:T(512)S(1)}, f32[1,512,128]{2,1,0:T(8,128)S(1)}) fusion(f32[2,512,128]{2,1,0:T(8,128)} %get-tuple-element.246, s32[]{:T(128)S(6)} %copy.112), kind=kLoop, calls=%fused_computation.63.clone.1 | loop fusion | flops 65024 | bytes 526340 | tf_op jit(solution)/shard_map/while/body/eval_jaxpr/reduce_sum | solution.py:16
  6.2 0.5 fusion.66
  6.7 0.4 copy-done.14
  7.0 0.5 fusion.67
  7.8 0.4 copy-done.4
  8.2 0.2 convolution_bitcast_fusion.2
  9.2 0.7 copy.81
  9.9 7.4 %all-to-all-start = ((bf16[16,1,8,512]{3,2,1,0:T(8,128)(2,1)}), bf16[16,1,8,512]{3,2,1,0:T(8,128)(2,1)S(1)}, u32[]{:S(2)}, u32[]{:S(2)}) async-start(bf16[16,1,8,512]{3,2,1,0:T(8,128)(2,1)} %bitcast.17), calls=%async_computation | async-start | bytes 262144 | tf_op jit(solution)/shard_map/all_to_all | solution.py:123
  17.3 0.3 fusion.38
  18.7 5.3 %all_gather.7 = bf16[32,768]{1,0:T(8,128)(2,1)S(1)} all-gather(bf16[8,768]{1,0:T(8,128)(2,1)S(1)} %convolution_convert_fusion.2), channel_id=1, replica_groups=mesh['parts'=2,'rows'=4,'cols'=4] {'rows'}, dimensions={0}, use_global_device_ids=true | all-gather | bytes 61440 | tf_op jit(solution)/shard_map/all_gather | solution.py:90
  24.5 0.3 fusion.39
  24.8 12.1 %pmax.7 = f32[16,32]{1,0:T(8,128)S(1)} all-reduce(f32[16,32]{1,0:T(8,128)S(1)} %get-tuple-element.139), channel_id=1, replica_groups=mesh['parts'=2,'rows'=4,'cols'=4] {'cols'}, use_global_device_ids=true, to_apply=%region_9.10 | all-reduce | flops 512 | bytes 4096 | tf_op jit(solution)/shard_map/pmax | solution.py:104
  37.0 13.2 %all-gather = bf16[64,32]{1,0:T(8,128)(2,1)S(1)} all-gather(bf16[16,32]{1,0:T(8,128)(2,1)S(1)} %fusion.24), channel_id=2, replica_groups=mesh['parts'=2,'rows'=4,'cols'=4] {'cols'}, dimensions={0}, use_global_device_ids=true | all-gather | bytes 5120 | tf_op jit(solution)/shard_map/all_gather | solution.py:11
  50.4 0.2 convolution_convert_fusion.1
  50.7 15.8 %psum.7 = bf16[32,384]{1,0:T(8,128)(2,1)S(1)} all-reduce(bf16[32,384]{1,0:T(8,128)(2,1)S(1)} %copy.89), channel_id=1, replica_groups=mesh['parts'=2,'rows'=4,'cols'=4] {'cols'}, use_global_device_ids=true, to_apply=%region_10.11 | all-reduce | flops 12288 | bytes 49152 | tf_op jit(solution)/shard_map/psum | solution.py:112
  67.2 1.0 %convolution_add_fusion.3 = f32[32,384]{1,0:T(8,128)} fusion(f32[32,384]{1,0:T(8,128)S(1)} %get-tuple-element.138, bf16[384,384]{1,0:T(8,128)(2,1)S(1)} %copy-done, bf16[32,384]{1,0:T(8,128)(2,1)S(1)} %multiply_convert_fusion.4, bf16[384,1536]{1,0:T(8,128)(2,1)S(1)} %copy-done.2, f32[32,384]{1,0:T(8,128)S(1)} %div.40, bf16[32,384]{1,0:T(8,128)(2,1)S(1)} %psum.7), kind=kOutput, calls=%fused_computation.36 | convolution fusion | flops 18972672 | bytes 786432 | tf_op jit(solution)/shard_map/dot_general | solution.py:118
  68.6 0.8 %add_add_fusion = f32[32,4,512]{2,1,0:T(4,128)} fusion(f32[32,4,512]{2,1,0:T(4,128)S(1)} %reshape.118, f32[32,4,512]{2,1,0:T(4,128)S(1)} %reshape.119, f32[512]{0:T(512)S(1)} %add.80), kind=kLoop, calls=%fused_computation.44 | loop fusion | flops 131072 | bytes 788480 | tf_op jit(solution)/shard_map/add | solution.py:128
  (98 shorter events, 4.9 us)
Async XLA Ops:
  0.6 66.6 %copy-start = (bf16[384,384]{1,0:T(8,128)(2,1)S(1)}, bf16[384,384]{1,0:T(8,128)(2,1)}, u32[]{:S(2)}) copy-start(bf16[384,384]{1,0:T(8,128)(2,1)} %param.29) | copy-start | bytes 884740
  0.7 1.4 %copy-start.1 = (bf16[128,1024]{1,0:T(8,128)(2,1)S(1)}, bf16[128,1024]{1,0:T(8,128)(2,1)}, u32[]{:S(2)}) copy-start(bf16[128,1024]{1,0:T(8,128)(2,1)} %get-tuple-element.248) | copy-start | bytes 786436 | tf_op jit(solution)/shard_map/while
  0.7 1.4 %copy-start.8 = (f32[128]{0:T(128)S(1)}, f32[128]{0:T(128)}, u32[]{:S(2)}) copy-start(f32[128]{0:T(128)} %get-tuple-element.247) | copy-start | bytes 1540 | tf_op jit(solution)/shard_map/while
  2.1 0.9 %copy-start.14 = (bf16[512,128]{1,0:T(8,128)(2,1)S(1)}, bf16[512,128]{1,0:T(8,128)(2,1)}, u32[]{:S(2)}) copy-start(bf16[512,128]{1,0:T(8,128)(2,1)} %get-tuple-element.249) | copy-start | bytes 393220 | tf_op jit(solution)/shard_map/while
  3.5 0.7 copy-start.4
  3.5 0.7 copy-start.7
  3.5 1.1 %copy-start.3 = (bf16[128,64]{0,1:T(8,128)(2,1)S(1)}, bf16[128,64]{0,1:T(8,128)(2,1)}, u32[]{:S(2)}) copy-start(bf16[128,64]{0,1:T(8,128)(2,1)} %get-tuple-element.252) | copy-start | bytes 49156 | tf_op jit(solution)/shard_map/while
  4.7 1.4 %copy-start.1 = (bf16[128,1024]{1,0:T(8,128)(2,1)S(1)}, bf16[128,1024]{1,0:T(8,128)(2,1)}, u32[]{:S(2)}) copy-start(bf16[128,1024]{1,0:T(8,128)(2,1)} %get-tuple-element.248) | copy-start | bytes 786436 | tf_op jit(solution)/shard_map/while
  4.8 1.4 %copy-start.8 = (f32[128]{0:T(128)S(1)}, f32[128]{0:T(128)}, u32[]{:S(2)}) copy-start(f32[128]{0:T(128)} %get-tuple-element.247) | copy-start | bytes 1540 | tf_op jit(solution)/shard_map/while
  6.1 0.9 %copy-start.14 = (bf16[512,128]{1,0:T(8,128)(2,1)S(1)}, bf16[512,128]{1,0:T(8,128)(2,1)}, u32[]{:S(2)}) copy-start(bf16[512,128]{1,0:T(8,128)(2,1)} %get-tuple-element.249) | copy-start | bytes 393220 | tf_op jit(solution)/shard_map/while
  7.5 0.7 copy-start.4
  7.5 0.7 copy-start.7
  7.5 1.1 %copy-start.3 = (bf16[128,64]{0,1:T(8,128)(2,1)S(1)}, bf16[128,64]{0,1:T(8,128)(2,1)}, u32[]{:S(2)}) copy-start(bf16[128,64]{0,1:T(8,128)(2,1)} %get-tuple-element.252) | copy-start | bytes 49156 | tf_op jit(solution)/shard_map/while
  8.8 9.4 %copy-start.13 = (f32[2,512,128]{2,1,0:T(8,128)}, f32[2,512,128]{2,1,0:T(8,128)S(1)}, u32[]{:S(2)}) copy-start(f32[2,512,128]{2,1,0:T(8,128)S(1)} %get-tuple-element.62) | copy-start | bytes 1572868
  8.8 8.5 %copy-start.5 = (f32[32,384]{1,0:T(8,128)S(1)}, f32[32,384]{1,0:T(8,128)}, u32[]{:S(2)}) copy-start(f32[32,384]{1,0:T(8,128)} %param.18) | copy-start | bytes 147460
  8.8 8.5 %copy-start.6 = (f32[32,384]{1,0:T(8,128)S(1)}, f32[32,384]{1,0:T(8,128)}, u32[]{:S(2)}) copy-start(f32[32,384]{1,0:T(8,128)} %param.26) | copy-start | bytes 147460
  8.8 8.5 %copy-start.11 = (s32[32]{0:T(128)S(1)}, s32[32]{0:T(128)}, u32[]{:S(2)}) copy-start(s32[32]{0:T(128)} %param.19) | copy-start | bytes 388
  8.8 9.3 %copy-start.9 = (f32[384]{0:T(512)S(1)}, f32[384]{0:T(512)}, u32[]{:S(2)}) copy-start(f32[384]{0:T(512)} %param.27) | copy-start | bytes 4612
  8.8 9.4 %copy-start.2 = (bf16[384,1536]{1,0:T(8,128)(2,1)S(1)}, bf16[384,1536]{1,0:T(8,128)(2,1)}, u32[]{:S(2)}) copy-start(bf16[384,1536]{1,0:T(8,128)(2,1)} %param.28) | copy-start | bytes 3538948
  9.9 58.3 %all-to-all-start = ((bf16[16,1,8,512]{3,2,1,0:T(8,128)(2,1)}), bf16[16,1,8,512]{3,2,1,0:T(8,128)(2,1)S(1)}, u32[]{:S(2)}, u32[]{:S(2)}) async-start(bf16[16,1,8,512]{3,2,1,0:T(8,128)(2,1)} %bitcast.17), calls=%async_computation | async-start | bytes 262144 | tf_op jit(solution)/shard_map/all_to_all | solution.py:123
  17.6 6.6 %copy-start.10 = (s32[4,4,1]{1,2,0:T(1,128)S(1)}, s32[4,4,1]{1,2,0:T(1,128)}, u32[]{:S(2)}) copy-start(s32[4,4,1]{1,2,0:T(1,128)} %param.20) | copy-start | bytes 196
  50.6 16.6 %copy-start.12 = (f32[64]{0:T(128)S(1)}, f32[64]{0:T(128)}, u32[]{:S(2)}) copy-start(f32[64]{0:T(128)} %param.31) | copy-start | bytes 772
